TPU v7x, 128 devices: a whole 4x4x4 slice. The times are simulated.
128 devices in a mesh: section: 4 (over y), dp: 2 (over core), expert: 16 (over x, z).
Axes of the slice: x: 4, y: 4, z: 4, core: 2. Of those that a mesh axis runs over, the one named last changes fastest.
Arguments:
- stashed: bfloat16 [4, 6144, 2048], P('section', ('dp', 'expert')), may hold values from -6 to 6
- expert_ids: int32 [4, 6144, 8], P('section', ('dp', 'expert')), may hold values from 0 to 63, all different within a row; in each aligned block of 192 rows (0 to 191, 192 to 383, ..., all dimensions but the last counted through in order) at most 48 rows name the same one
- route_probs: float32 [4, 6144, 8], P('section', ('dp', 'expert')), may hold values from 0.02 to 1
- w_gate: bfloat16 [4, 64, 2048, 768], P('section', ('dp', 'expert')), may hold values from -0.125 to 0.125
- w_up: bfloat16 [4, 64, 2048, 768], P('section', ('dp', 'expert')), may hold values from -0.125 to 0.125
- w_down: bfloat16 [4, 64, 768, 2048], P('section', ('dp', 'expert')), may hold values from -0.21875 to 0.21875
Outputs:
- handed: bfloat16 [4, 6144, 2048], P('section', ('dp', 'expert'))
- balance: float32 [4], P('section')
Inputs may be any that keep to these rules, and one draw needn't show every extreme that they name: `expert_ids`: each token names 8 different experts; among the tokens of one device (aligned blocks of 192 tokens) no expert is named more than 48 times, and in every draw some expert is named exactly 48 times in some block.
All inputs are finite; a program needn't handle non-finite values.
Results may differ from a plain program's by a relative error of at most 0.0032.
Values may be sent and summed in bfloat16 or wider, within the bound.
No kernel may reach another device: no remote copies, remote signals or barrier semaphores. Data moves between devices by JAX's collectives and lax.ppermute only.
A program may use at most 128 MiB of HBM per device.

v0:
```python
import jax
import jax.numpy as jnp
from jax import lax
from jax.sharding import PartitionSpec as P


def passed_along(value, axis, steps):
    count = lax.axis_size(axis)
    pairs = [(source, (source + steps) % count) for source in range(count)]
    return lax.ppermute(value, axis, pairs)


def expert_rows(received, gate_w, up_w, down_w, form_in, form_out):
    gate_act = jnp.einsum(form_in, received, gate_w, preferred_element_type=jnp.float32)
    up_act = jnp.einsum(form_in, received, up_w, preferred_element_type=jnp.float32)
    hidden = (jax.nn.silu(gate_act) * up_act).astype(jnp.bfloat16)
    return jnp.einsum(form_out, hidden, down_w, preferred_element_type=jnp.float32).astype(
        jnp.bfloat16
    )


def per_device(stashed, expert_ids, route_probs, w_gate, w_up, w_down):
    tokens_in = stashed[0]
    choice_ids = expert_ids[0]
    probs = route_probs[0]
    gate_w = w_gate[0]
    up_w = w_up[0]
    down_w = w_down[0]
    expert_count = lax.axis_size("expert")
    dp_count = lax.axis_size("dp")
    local_count = gate_w.shape[0]
    all_experts = dp_count * expert_count * local_count
    token_count, top_count = choice_ids.shape
    model_width = tokens_in.shape[1]
    capacity = 2 * token_count * top_count // all_experts
    inputs = tokens_in.astype(jnp.float32)
    normed = (inputs * lax.rsqrt(jnp.mean(inputs * inputs, axis=-1, keepdims=True) + 1e-06)).astype(
        jnp.bfloat16
    )
    flat_ids = choice_ids.reshape(-1)
    labels = jnp.arange(all_experts, dtype=jnp.int32)
    onehot = (flat_ids[:, None] == labels[None, :]).astype(jnp.int32)
    running = jnp.cumsum(onehot, axis=0)
    position = jnp.sum(running * onehot, axis=1) - 1
    slot_rows = flat_ids * capacity + position
    sent_rows = (
        jnp.zeros((all_experts * capacity, model_width), jnp.bfloat16)
        .at[slot_rows]
        .set(jnp.repeat(normed, top_count, axis=0))
    )
    arranged = sent_rows.reshape(dp_count * expert_count, local_count, capacity, model_width)
    received = lax.all_to_all(arranged, ("dp", "expert"), split_axis=0, concat_axis=0, tiled=True)
    result = expert_rows(received, gate_w, up_w, down_w, "secd,edf->secf", "secf,efd->secd")
    returned = lax.all_to_all(result, ("dp", "expert"), split_axis=0, concat_axis=0, tiled=True)
    picked = returned.reshape(all_experts * capacity, model_width)[slot_rows]
    picked = picked.reshape(token_count, top_count, model_width).astype(jnp.float32)
    weights = probs / jnp.sum(probs, axis=-1, keepdims=True)
    mixture = jnp.sum(weights[:, :, None] * picked, axis=1)
    layer_out = (inputs + mixture).astype(jnp.bfloat16)
    counts = jnp.sum(onehot, axis=0).astype(jnp.float32)
    mass = jnp.dot(weights.reshape(-1), onehot.astype(jnp.float32), precision=lax.Precision.HIGHEST)
    counts_all, mass_all = lax.psum((counts, mass), ("dp", "expert"))
    tokens_all = token_count * dp_count * expert_count
    loss = all_experts * jnp.sum(counts_all / (tokens_all * top_count) * (mass_all / tokens_all))
    handed = passed_along(layer_out, "section", 1)
    return (handed[None], loss.reshape(1))


def solution(mesh):
    placed = (
        P("section", ("dp", "expert"), None),
        P("section", ("dp", "expert"), None),
        P("section", ("dp", "expert"), None),
        P("section", ("dp", "expert"), None, None),
        P("section", ("dp", "expert"), None, None),
        P("section", ("dp", "expert"), None, None),
    )
    return jax.shard_map(
        per_device,
        mesh=mesh,
        in_specs=placed,
        out_specs=(P("section", ("dp", "expert"), None), P("section")),
        check_vma=False,
    )
```

profile of v0, /device:TPU:2, one launch (start us, length us, event | category | flops | bytes accessed | tf_op | source)
XLA Modules:
  0.0 558.4 jit_solution(3848793365307210415)
XLA Ops:
  0.6 0.8 copy.21
  1.4 0.1 eq.29
  1.5 0.1 eq.25
  1.7 0.7 broadcast_multiply_fusion
  2.4 18.1 %reduce-window.6 = s32[64,12,128]{2,1,0:T(8,128)S(1)} reduce-window(s32[64,12,128]{2,1,0:T(8,128)S(1)} %fusion.29, s32[]{:T(128)} %constant.9.clone.1), window={size=1x1x128 pad=0_0x0_0x127_0}, to_apply=%region_1.0 | reduce-window | flops 12484608 | bytes 786436 | tf_op jit(solution)/shard_map/reduce-window
  20.5 0.2 slice.10
  20.7 0.3 copy.23
  21.0 0.1 copy.24
  21.1 0.2 broadcast_add_fusion
  21.3 0.2 convert_reduce_fusion
  21.6 0.1 copy.20
  21.7 0.1 mul.51
  21.8 1.4 fusion.26
  23.2 1.3 fusion.27
  24.5 16.3 %scatter_custom_fusion = bf16[3072,2048]{1,0:T(8,128)(2,1)} fusion(s32[1536]{0:T(1024)S(1)} %fusion.33, bf16[]{:T(256)} %constant.8.clone.1, bf16[192,2048]{1,0:T(8,128)(2,1)S(1)} %fusion.27), kind=kCustom, calls=%fused_computation.19 | custom fusion | bytes 13369346 | tf_op jit(solution)/shard_map/scatter | solution.py:49
  40.9 149.1 %all_to_all.10 = bf16[32,2,48,2048]{3,2,1,0:T(8,128)(2,1)S(1)} all-to-all(bf16[32,2,48,2048]{3,2,1,0:T(8,128)(2,1)} %bitcast.78), channel_id=1, replica_groups=mesh['section'=4,'dp'=2,'expert'=16] {'dp','expert'}, dimensions={0} | all-to-all | bytes 25165824 | tf_op jit(solution)/shard_map/all_to_all | solution.py:52
  189.9 0.0 copy-start
  189.9 4.5 copy-done
  194.4 14.1 %fusion.1 = f32[2,32,48,768]{3,2,1,0:T(8,128)} fusion(bf16[32,2,48,2048]{3,2,1,0:T(8,128)(2,1)S(1)} %all_to_all.10, bf16[1,2,2048,768]{3,2,1,0:T(8,128)(2,1)} %param.10), kind=kOutput, calls=%fused_computation.5 | convolution fusion | flops 9663676416 | bytes 28311552 | tf_op jit(solution)/shard_map/secd,edf->secf/dot_general | solution.py:15
  208.4 29.3 %convert_bitcast_fusion = bf16[32,2,48,2048]{3,2,0,1:T(8,128)(2,1)} fusion(bf16[1,2,768,2048]{3,2,1,0:T(8,128)(2,1)} %param.11, f32[2,32,48,768]{3,2,1,0:T(8,128)} %fusion.1, bf16[32,2,48,2048]{3,2,1,0:T(8,128)(2,1)} %copy-done, bf16[1,2,2048,768]{3,2,1,0:T(8,128)(2,1)} %param.9), kind=kOutput, calls=%fused_computation.4 | convolution fusion | flops 19347800064 | bytes 47185920 | tf_op jit(solution)/shard_map/secf,efd->secd/dot_general | solution.py:17
  237.8 10.8 %copy.27 = bf16[32,2,48,2048]{3,2,1,0:T(8,128)(2,1)} copy(bf16[32,2,48,2048]{3,2,0,1:T(8,128)(2,1)} %convert_bitcast_fusion) | data formatting | bytes 25165824 | tf_op jit(solution)/shard_map/convert_element_type | solution.py:17
  248.6 0.0 copy-start.2
  248.6 5.4 all-to-all-start.1
  254.0 0.0 copy-done.2
  254.1 0.1 copy.19
  254.2 194.4 %all-to-all-done.1 = bf16[32,2,48,2048]{3,2,1,0:T(8,128)(2,1)} async-done(((bf16[32,2,48,2048]{3,2,1,0:T(8,128)(2,1)}), bf16[32,2,48,2048]{3,2,1,0:T(8,128)(2,1)}, u32[]{:S(2)}, u32[]{:S(2)}) %all-to-all-start.1) | async-done | bytes 12582944 | tf_op jit(solution)/shard_map/all_to_all | solution.py:54
  448.6 0.0 copy-start.1
  448.6 19.0 %gather_fusion = bf16[1536,2048]{1,0:T(8,128)(2,1)} fusion(bf16[3072,2048]{1,0:T(8,128)(2,1)} %bitcast.19, s32[2048]{0:T(1024)S(1)} %pad_clamp_fusion), kind=kCustom, calls=%fused_computation | custom fusion | bytes 12589056 | tf_op jit(solution)/shard_map/gather | solution.py:55
  467.6 9.2 %fusion = f32[192,2048]{1,0:T(8,128)S(1)} fusion(bf16[1536,2048]{1,0:T(8,128)(2,1)} %gather_fusion, f32[192,8]{1,0:T(8,128)S(1)} %copy.19), kind=kLoop, calls=%fused_computation.3 | loop fusion | flops 9043968 | bytes 7870464 | tf_op jit(solution)/shard_map/reduce_sum | solution.py:58
  476.9 0.0 copy-done.1
  476.9 0.2 fusion.28
  477.1 1.7 collective-permute-start
  478.7 0.1 copy.28
  478.9 0.1 div.39.clone
  478.9 0.1 div.46
  479.1 0.1 squeeze.19
  479.2 0.4 convolution_bitcast_fusion
  479.6 75.5 %all-reduce = (f32[64]{0:T(128)S(1)}, f32[64]{0:T(128)S(1)}) all-reduce(f32[64]{0:T(128)S(1)} %convolution_bitcast_fusion, f32[64]{0:T(128)S(1)} %convert_element_type.51), channel_id=1, replica_groups=mesh['section'=4,'dp'=2,'expert'=16] {'dp','expert'}, use_global_device_ids=true, to_apply=%region_9.10 | all-reduce | flops 128 | bytes 1024 | tf_op jit(solution)/shard_map/psum | solution.py:62
  555.1 0.6 multiply_reduce_fusion
  556.4 0.0 collective-permute-done
  556.4 0.9 copy.44
  (11 shorter events, 0.2 us)
Async XLA Ops:
  189.9 4.5 copy-start
  248.6 5.5 copy-start.2
  248.6 200.0 %all-to-all-start.1 = ((bf16[32,2,48,2048]{3,2,1,0:T(8,128)(2,1)}), bf16[32,2,48,2048]{3,2,1,0:T(8,128)(2,1)}, u32[]{:S(2)}, u32[]{:S(2)}) async-start(bf16[32,2,48,2048]{3,2,1,0:T(8,128)(2,1)} %copy.27), calls=%async_computation.1 | async-start | bytes 25165824 | tf_op jit(solution)/shard_map/all_to_all | solution.py:54
  448.6 28.2 %copy-start.1 = (bf16[1,192,2048]{2,1,0:T(8,128)(2,1)S(1)}, bf16[1,192,2048]{2,1,0:T(8,128)(2,1)}, u32[]{:S(2)}) copy-start(bf16[1,192,2048]{2,1,0:T(8,128)(2,1)} %param.6) | copy-start | bytes 2359300
  477.1 79.3 %collective-permute-start = (bf16[192,2048]{1,0:T(8,128)(2,1)S(1)}, bf16[192,2048]{1,0:T(8,128)(2,1)S(1)}, u32[]{:S(2)}, u32[]{:S(2)}) collective-permute-start(bf16[192,2048]{1,0:T(8,128)(2,1)S(1)} %fusion.28), channel_id=1, source_target_pairs={{0,32},{32,64},{64,96},{96,0},{1,33},{33,65},{65,97},{97,1},{2,34}... | collective-permute-start | bytes 2359304 | tf_op jit(solution)/shard_map/ppermute | solution.py:10
where the time goes:
time: 559 us; the launch traced here: 558 us
  blocking collectives  225 us (40%)
  waiting for transfers between devices  194 us (35%)
  local copies, waits for them, and re-layouts  53.8 us (10%)
  matrix products  43.8 us (8%)
  other arithmetic  32.1 us (6%)
  starting transfers between devices  7.09 us (1%)
    all_to_all x1, waiting for transfers between devices, per_device(): lax.all_to_all(result, ('dp', 'expert'), split_axis=0, concat_axis=0, til...  194 us
    all_to_all x1, blocking collectives, per_device(): lax.all_to_all(arranged, ('dp', 'expert'), split_axis=0, concat_axis=0, t...  149 us
    psum x1, blocking collectives, per_device(): counts_all, mass_all = lax.psum((counts, mass), ('dp', 'expert'))  75.5 us
    dot_general x1, matrix products, expert_rows(): jnp.einsum(form_out, hidden, down_w, preferred_element_type=jnp.float32)  29.3 us
    gather x1, local copies, waits for them, and re-layouts, per_device(): picked = returned.reshape(all_experts * capacity, model_width)[slot_rows]  19 us
    another operation x3, other arithmetic  18.4 us
    scatter x1, local copies, waits for them, and re-layouts, per_device(): sent_rows = jnp.zeros((all_experts * capacity, model_width), jnp.bfloat16...  16.3 us
    dot_general x1, matrix products, expert_rows(): jnp.einsum(form_in, received, up_w, preferred_element_type=jnp.float32)  14.1 us
  transfers between devices with their start and end apart: 2, of which 1 were waited for; matrix products, arithmetic and copies ran while one was open for 0% of the time, Pallas kernels for 0%

commit v1 on v0

--- a/solution.py
+++ b/solution.py
@@ -59,7 +59,8 @@
     layer_out = (inputs + mixture).astype(jnp.bfloat16)
     counts = jnp.sum(onehot, axis=0).astype(jnp.float32)
     mass = jnp.dot(weights.reshape(-1), onehot.astype(jnp.float32), precision=lax.Precision.HIGHEST)
-    counts_all, mass_all = lax.psum((counts, mass), ("dp", "expert"))
+    plan_loads = lambda frame_in: lax.psum(lax.psum(frame_in, "expert"), "dp")
+    counts_all, mass_all = plan_loads((counts, mass))
     tokens_all = token_count * dp_count * expert_count
     loss = all_experts * jnp.sum(counts_all / (tokens_all * top_count) * (mass_all / tokens_all))
     handed = passed_along(layer_out, "section", 1)

time: 559 us -> 534 us (0.955)
  blocking collectives: 225 us -> 198 us
    psum x1 -> x2, blocking collectives: 75.5 us -> 48.6 us  [per_device(): plan_loads = lambda frame_in: lax.psum(lax.psum(frame_in, 'expert'), 'dp')]
where the time goes in v1:
time: 534 us; the launch traced here: 532 us
  blocking collectives  198 us (37%)
  waiting for transfers between devices  194 us (36%)
  local copies, waits for them, and re-layouts  53.8 us (10%)
  matrix products  43.8 us (8%)
  other arithmetic  32.1 us (6%)
  starting transfers between devices  7.09 us (1%)
    all_to_all x1, waiting for transfers between devices, per_device(): lax.all_to_all(result, ('dp', 'expert'), split_axis=0, concat_axis=0, til...  194 us
    all_to_all x1, blocking collectives, per_device(): lax.all_to_all(arranged, ('dp', 'expert'), split_axis=0, concat_axis=0, t...  149 us
    psum x2, blocking collectives, per_device(): plan_loads = lambda frame_in: lax.psum(lax.psum(frame_in, 'expert'), 'dp')  48.6 us
    dot_general x1, matrix products, expert_rows(): jnp.einsum(form_out, hidden, down_w, preferred_element_type=jnp.float32)  29.3 us
    gather x1, local copies, waits for them, and re-layouts, per_device(): picked = returned.reshape(all_experts * capacity, model_width)[slot_rows]  19 us
    another operation x3, other arithmetic  18.4 us
    scatter x1, local copies, waits for them, and re-layouts, per_device(): sent_rows = jnp.zeros((all_experts * capacity, model_width), jnp.bfloat16...  16.3 us
    dot_general x1, matrix products, expert_rows(): jnp.einsum(form_in, received, up_w, preferred_element_type=jnp.float32)  14.1 us
  transfers between devices with their start and end apart: 2, of which 1 were waited for; matrix products, arithmetic and copies ran while one was open for 0% of the time, Pallas kernels for 0%

profile of v1, /device:TPU:2, one launch (start us, length us, event | category | flops | bytes accessed | tf_op | source)
XLA Modules:
  0.0 531.5 jit_solution(4934498667778157854)
XLA Ops:
  0.6 0.8 copy.21
  1.4 0.1 eq.29
  1.5 0.1 eq.25
  1.7 0.7 broadcast_multiply_fusion
  2.4 18.1 %reduce-window.6 = s32[64,12,128]{2,1,0:T(8,128)S(1)} reduce-window(s32[64,12,128]{2,1,0:T(8,128)S(1)} %fusion.29, s32[]{:T(128)} %constant.9.clone.1), window={size=1x1x128 pad=0_0x0_0x127_0}, to_apply=%region_1.0 | reduce-window | flops 12484608 | bytes 786436 | tf_op jit(solution)/shard_map/reduce-window
  20.5 0.2 slice.10
  20.7 0.3 copy.23
  21.0 0.1 copy.24
  21.1 0.2 broadcast_add_fusion
  21.3 0.2 convert_reduce_fusion
  21.6 0.1 copy.20
  21.7 0.1 mul.51
  21.8 1.4 fusion.26
  23.2 1.3 fusion.27
  24.5 16.3 %scatter_custom_fusion = bf16[3072,2048]{1,0:T(8,128)(2,1)} fusion(s32[1536]{0:T(1024)S(1)} %fusion.33, bf16[]{:T(256)} %constant.8.clone.1, bf16[192,2048]{1,0:T(8,128)(2,1)S(1)} %fusion.27), kind=kCustom, calls=%fused_computation.19 | custom fusion | bytes 13369346 | tf_op jit(solution)/shard_map/scatter | solution.py:49
  40.9 149.1 %all_to_all.10 = bf16[32,2,48,2048]{3,2,1,0:T(8,128)(2,1)S(1)} all-to-all(bf16[32,2,48,2048]{3,2,1,0:T(8,128)(2,1)} %bitcast.78), channel_id=1, replica_groups=mesh['section'=4,'dp'=2,'expert'=16] {'dp','expert'}, dimensions={0} | all-to-all | bytes 25165824 | tf_op jit(solution)/shard_map/all_to_all | solution.py:52
  189.9 0.0 copy-start
  189.9 4.5 copy-done
  194.4 14.1 %fusion.1 = f32[2,32,48,768]{3,2,1,0:T(8,128)} fusion(bf16[32,2,48,2048]{3,2,1,0:T(8,128)(2,1)S(1)} %all_to_all.10, bf16[1,2,2048,768]{3,2,1,0:T(8,128)(2,1)} %param.10), kind=kOutput, calls=%fused_computation.5 | convolution fusion | flops 9663676416 | bytes 28311552 | tf_op jit(solution)/shard_map/secd,edf->secf/dot_general | solution.py:15
  208.4 29.3 %convert_bitcast_fusion = bf16[32,2,48,2048]{3,2,0,1:T(8,128)(2,1)} fusion(bf16[1,2,768,2048]{3,2,1,0:T(8,128)(2,1)} %param.11, f32[2,32,48,768]{3,2,1,0:T(8,128)} %fusion.1, bf16[32,2,48,2048]{3,2,1,0:T(8,128)(2,1)} %copy-done, bf16[1,2,2048,768]{3,2,1,0:T(8,128)(2,1)} %param.9), kind=kOutput, calls=%fused_computation.4 | convolution fusion | flops 19347800064 | bytes 47185920 | tf_op jit(solution)/shard_map/secf,efd->secd/dot_general | solution.py:17
  237.8 10.8 %copy.27 = bf16[32,2,48,2048]{3,2,1,0:T(8,128)(2,1)} copy(bf16[32,2,48,2048]{3,2,0,1:T(8,128)(2,1)} %convert_bitcast_fusion) | data formatting | bytes 25165824 | tf_op jit(solution)/shard_map/convert_element_type | solution.py:17
  248.6 0.0 copy-start.2
  248.6 5.4 %all-to-all-start.1 = ((bf16[32,2,48,2048]{3,2,1,0:T(8,128)(2,1)}), bf16[32,2,48,2048]{3,2,1,0:T(8,128)(2,1)}, u32[]{:S(2)}, u32[]{:S(2)}) async-start(bf16[32,2,48,2048]{3,2,1,0:T(8,128)(2,1)} %copy.27), calls=%async_computation.1 | async-start | bytes 25165824 | tf_op jit(solution)/shard_map/all_to_all | solution.py:54
  254.0 0.0 copy-done.2
  254.1 0.1 copy.19
  254.2 194.4 %all-to-all-done.1 = bf16[32,2,48,2048]{3,2,1,0:T(8,128)(2,1)} async-done(((bf16[32,2,48,2048]{3,2,1,0:T(8,128)(2,1)}), bf16[32,2,48,2048]{3,2,1,0:T(8,128)(2,1)}, u32[]{:S(2)}, u32[]{:S(2)}) %all-to-all-start.1) | async-done | bytes 12582944 | tf_op jit(solution)/shard_map/all_to_all | solution.py:54
  448.6 0.0 copy-start.1
  448.6 19.0 %gather_fusion = bf16[1536,2048]{1,0:T(8,128)(2,1)} fusion(bf16[3072,2048]{1,0:T(8,128)(2,1)} %bitcast.19, s32[2048]{0:T(1024)S(1)} %pad_clamp_fusion), kind=kCustom, calls=%fused_computation | custom fusion | bytes 12589056 | tf_op jit(solution)/shard_map/gather | solution.py:55
  467.6 9.2 %fusion = f32[192,2048]{1,0:T(8,128)S(1)} fusion(bf16[1536,2048]{1,0:T(8,128)(2,1)} %gather_fusion, f32[192,8]{1,0:T(8,128)S(1)} %copy.19), kind=kLoop, calls=%fused_computation.3 | loop fusion | flops 9043968 | bytes 7870464 | tf_op jit(solution)/shard_map/reduce_sum | solution.py:58
  476.9 0.0 copy-done.1
  476.9 0.2 fusion.28
  477.1 1.7 collective-permute-start
  478.7 0.1 copy.28
  478.9 0.1 div.39.clone
  478.9 0.1 div.46
  479.1 0.1 squeeze.19
  479.2 0.4 convolution_bitcast_fusion
  479.6 46.2 %all-reduce = (f32[64]{0:T(128)S(1)}, f32[64]{0:T(128)S(1)}) all-reduce(f32[64]{0:T(128)S(1)} %convolution_bitcast_fusion, f32[64]{0:T(128)S(1)} %convert_element_type.51), channel_id=1, replica_groups=mesh['section'=4,'dp'=2,'expert'=16] {'expert'}, use_global_device_ids=true, to_apply=%region_10.11 | all-reduce | flops 128 | bytes 1024 | tf_op jit(solution)/shard_map/psum | solution.py:62
  525.8 2.5 all-reduce.1
  528.2 0.6 multiply_reduce_fusion
  529.5 0.0 collective-permute-done
  529.5 0.9 copy.44
  (11 shorter events, 0.2 us)
Async XLA Ops:
  189.9 4.5 copy-start
  248.6 5.5 %copy-start.2 = (f32[1,192,8]{1,2,0:T(8,128)S(1)}, f32[1,192,8]{1,2,0:T(8,128)}, u32[]{:S(2)}) copy-start(f32[1,192,8]{1,2,0:T(8,128)} %param.8) | copy-start | bytes 18436
  248.6 200.0 %all-to-all-start.1 = ((bf16[32,2,48,2048]{3,2,1,0:T(8,128)(2,1)}), bf16[32,2,48,2048]{3,2,1,0:T(8,128)(2,1)}, u32[]{:S(2)}, u32[]{:S(2)}) async-start(bf16[32,2,48,2048]{3,2,1,0:T(8,128)(2,1)} %copy.27), calls=%async_computation.1 | async-start | bytes 25165824 | tf_op jit(solution)/shard_map/all_to_all | solution.py:54
  448.6 28.2 %copy-start.1 = (bf16[1,192,2048]{2,1,0:T(8,128)(2,1)S(1)}, bf16[1,192,2048]{2,1,0:T(8,128)(2,1)}, u32[]{:S(2)}) copy-start(bf16[1,192,2048]{2,1,0:T(8,128)(2,1)} %param.6) | copy-start | bytes 2359300
  477.1 52.4 %collective-permute-start = (bf16[192,2048]{1,0:T(8,128)(2,1)S(1)}, bf16[192,2048]{1,0:T(8,128)(2,1)S(1)}, u32[]{:S(2)}, u32[]{:S(2)}) collective-permute-start(bf16[192,2048]{1,0:T(8,128)(2,1)S(1)} %fusion.28), channel_id=1, source_target_pairs={{0,32},{32,64},{64,96},{96,0},{1,33},{33,65},{65,97},{97,1},{2,34}... | collective-permute-start | bytes 2359304 | tf_op jit(solution)/shard_map/ppermute | solution.py:10
